TPU v7x, 256 devices: a whole 4x4x8 slice. The times are simulated.
256 devices in a mesh: chan: 32 (over y_lo, z, core), win: 8 (over y_hi, x).
Axes of the slice: x: 4, y: 4 (y_hi: 2, y_lo: 2; y = y_hi * 2 + y_lo), z: 8, core: 2. Of those that a mesh axis runs over, the one named last changes fastest.
Arguments:
- traces: bfloat16 [96, 2048, 4096], P('win', 'chan'), may hold values from -6 to 6
- quality: int32 [2048], P('chan'), may hold values 0 or 1
- fold_block: int32 [2048, 1], replicated, may hold values from 0 to 31; in each aligned block of 64 rows (0 to 63, 64 to 127, ...) at most 8 rows name the same one
- fold_offset: int32 [2048], replicated, may hold values from 0 to 63
Outputs:
- neighbour_lags: float32 [2048, 64, 256], P(('chan', 'win'))
- fold_lags: float32 [2048, 256], P(('chan', 'win'))
Inputs may be any that keep to these rules, and one draw needn't show every extreme that they name: `fold_block`: within each aligned block of 64 channels no block number appears more than 8 times.
All inputs are finite; a program needn't handle non-finite values. No bound on the sum of `quality` on one device may be relied on, other than what follows from the above.
Results may differ from a plain program's by a relative error of at most 0.0052.
Values may be sent and summed in bfloat16 or wider, within the bound.
A program may use at most 128 MiB of HBM per device.

v0:
```python
import math

import jax
import jax.numpy as jnp
import ml_dtypes
import numpy as np
from jax import lax
from jax.experimental import pallas as pl
from jax.experimental.pallas import tpu as pltpu
from jax.sharding import PartitionSpec as P

F = 256
BAND_LO = 32
NLAG = 256
REACH = 64
L = 4096
CH_DEV = 64
CHANNELS = 2048
WINDOWS = 96
N_CHAN = 32
N_WIN = 8
DEVICES = N_CHAN * N_WIN
WIN_DEV = WINDOWS // N_WIN
ROWS = CHANNELS // DEVICES
SMOOTH = 4
STEP = 128
GROUP = 4
CHUNKS = WIN_DEV // GROUP
LANES = GROUP * CH_DEV
MESH = pl.DeviceIdType.MESH
BF16 = jnp.bfloat16
F32 = jnp.float32


def forward_phases():
    frequency = np.arange(F, dtype=np.int64)[:, None] + BAND_LO
    fine = np.arange(STEP, dtype=np.int64)
    coarse = np.arange(L // STEP, dtype=np.int64) * STEP
    tables = []
    for steps in (fine, coarse):
        angles = (frequency * steps[None, :] % L).astype(np.float64) * (2.0 * math.pi / L)
        tables += [np.cos(angles), np.sin(angles)]
    joined = np.concatenate(tables, axis=1).astype(np.float32)
    return np.pad(joined, ((0, 0), (0, -joined.shape[1] % 128)))


def inverse_halves():
    shifts = np.arange(NLAG, dtype=np.int64)[None, :] + NLAG // 2
    frequency = np.arange(F, dtype=np.int64)[:, None] + BAND_LO
    angles = (frequency * shifts % NLAG).astype(np.float64) * (2.0 * math.pi / NLAG)
    factor = 1.0 / math.sqrt(F * WINDOWS)
    halves = []
    for part in (np.cos(angles) * factor, -np.sin(angles) * factor):
        high = part.astype(np.float32).astype(ml_dtypes.bfloat16)
        low = (part - high.astype(np.float64)).astype(np.float32).astype(ml_dtypes.bfloat16)
        halves += [high, low]
    return np.stack(halves)


def kernel(
    x_hbm, q_ref, idx_ref, phase_hbm, inverse_hbm, near_ref, fold_ref,
    xs, phase, inverse, table, energy, staged, sent, got, x, chosen_rows, band, folded, band_in, folded_in, flat, flat_fold, lag_in, turned_fold,
    in_sems, own_sem, send_sem, recv_sem, band_send, band_recv, fold_send, fold_recv,
):
    chan, win = lax.axis_index("chan"), lax.axis_index("win")
    me = chan * N_WIN + win

    def place(other):
        return (other // N_WIN, lax.rem(other, N_WIN))

    phase_copy = pltpu.make_async_copy(phase_hbm, phase, in_sems.at[CHUNKS])
    phase_copy.start()
    x_copies = [
        pltpu.make_async_copy(x_hbm.at[pl.ds(i * LANES, LANES)], xs.at[i], in_sems.at[i])
        for i in range(CHUNKS)
    ]
    for copy in x_copies:
        copy.start()
    inverse_copy = pltpu.make_async_copy(inverse_hbm, inverse, in_sems.at[CHUNKS + 1])
    inverse_copy.start()

    barrier = pltpu.get_barrier_semaphore()

    def greet(step, _):
        other = lax.rem(me + step, DEVICES)
        pl.semaphore_signal(barrier, inc=1, device_id=place(other), device_id_type=MESH)
        return 0

    lax.fori_loop(1, DEVICES, greet, 0)

    phase_copy.wait()
    coarse_at = 2 * STEP
    blocks = L // STEP
    fine_cos, fine_sin = phase[:, 0:STEP], phase[:, STEP : 2 * STEP]
    for block in range(blocks):
        cos_b = phase[:, coarse_at + block : coarse_at + block + 1]
        sin_b = phase[:, coarse_at + blocks + block : coarse_at + blocks + block + 1]
        lanes = slice(block * STEP, (block + 1) * STEP)
        table[0:F, lanes] = (fine_cos * cos_b - fine_sin * sin_b).astype(BF16)
        table[F : 2 * F, lanes] = (-fine_sin * cos_b - fine_cos * sin_b).astype(BF16)
    energy[0:8, :] = jnp.zeros((8, LANES), F32)
    energy[8 + F : 16 + F, :] = jnp.zeros((8, LANES), F32)

    low = lax.broadcasted_iota(jnp.int32, (F, 128), 1) < CH_DEV
    for i in range(CHUNKS):
        x_copies[i].wait()
        spectra = lax.dot_general(
            table[...], xs[i], (((1,), (1,)), ((), ())), preferred_element_type=F32
        )
        re, im = spectra[0:F], spectra[F : 2 * F]
        power = re * re + im * im
        energy[8 : 8 + F, :] = power
        smooth = power
        for shift in range(1, SMOOTH + 1):
            smooth = smooth + (
                energy[8 - shift : 8 - shift + F, :] + energy[8 + shift : 8 + shift + F, :]
            )
        water = jnp.sum(power, axis=0, keepdims=True) * (1.0 / F)
        scaling = lax.rsqrt(smooth * (1.0 / (2 * SMOOTH + 1)) + 0.1 * water + 1e-06) * q_ref[...]
        re, im = re * scaling, im * scaling
        for pair in range(GROUP // 2):
            re_p = re[:, pair * 128 : pair * 128 + 128]
            im_p = im[:, pair * 128 : pair * 128 + 128]
            first = jnp.where(low, re_p, pltpu.roll(im_p, CH_DEV, 1))
            second = jnp.where(low, pltpu.roll(re_p, CH_DEV, 1), im_p)
            staged[pl.ds(2 * pair, F, stride=GROUP), :] = first
            staged[pl.ds(2 * pair + 1, F, stride=GROUP), :] = second
        sent[:, i] = staged[...].reshape(F, GROUP, 128).astype(BF16)

    pl.semaphore_wait(barrier, DEVICES - 1)
    own_copy = pltpu.make_async_copy(sent.at[me], got.at[me], own_sem)
    own_copy.start()

    def send_spectra(step, _):
        other = lax.rem(me + step, DEVICES)
        pltpu.make_async_remote_copy(
            sent.at[other], got.at[me], send_sem, recv_sem,
            device_id=place(other), device_id_type=MESH,
        ).start()
        return 0

    lax.fori_loop(1, DEVICES, send_spectra, 0)
    own_copy.wait()

    def all_of(source, target, send, recv):
        some = pl.ds(0, DEVICES - 1)
        return pltpu.make_async_remote_copy(
            source.at[some], target.at[some], send, recv, device_id=place(lax.rem(me + 1, DEVICES)), device_id_type=MESH
        )

    spectra_copies = all_of(sent, got, send_sem, recv_sem)
    spectra_copies.wait_recv()

    low_w = lax.broadcasted_iota(jnp.int32, (WINDOWS, 128), 1) < CH_DEV

    def unpack(m, _):
        even = got[pl.ds(2 * N_WIN * m, N_WIN)].astype(F32).reshape(WINDOWS, 128)
        odd = got[pl.ds(2 * N_WIN * m + N_WIN, N_WIN)].astype(F32).reshape(WINDOWS, 128)
        lanes = pl.ds(pl.multiple_of(m * 128, 128), 128)
        x[0:WINDOWS, lanes] = jnp.where(low_w, even, pltpu.roll(odd, CH_DEV, 1)).astype(BF16)
        x[WINDOWS : 2 * WINDOWS, lanes] = jnp.where(low_w, pltpu.roll(even, CH_DEV, 1), odd).astype(BF16)
        return 0

    lax.fori_loop(0, N_CHAN // 2, unpack, 0)
    x[:, CHANNELS : CHANNELS + 128] = jnp.zeros((2 * WINDOWS, 128), BF16)

    low_1 = lax.broadcasted_iota(jnp.int32, (2, 128), 1) < CH_DEV

    def fold_block(g, _):
        lanes = pl.ds(pl.multiple_of(g * 256, 256), 256)
        wanted = idx_ref[:, lanes]
        rows = lax.broadcasted_iota(jnp.int32, (CHANNELS, 256), 0)
        chosen_rows[...] = jnp.where(rows == wanted, 1.0, 0.0).astype(BF16)
        partner = jnp.dot(x[:, 0:CHANNELS], chosen_rows[...], preferred_element_type=F32)
        own = x[:, lanes].astype(F32)
        re_a, im_a = own[:WINDOWS], own[WINDOWS:]
        re_b, im_b = partner[:WINDOWS], partner[WINDOWS:]
        re_c = jnp.sum(re_a * re_b + im_a * im_b, axis=0, keepdims=True)
        im_c = jnp.sum(im_a * re_b - re_a * im_b, axis=0, keepdims=True)
        re_c = jnp.broadcast_to(re_c, (2, 256))
        im_c = jnp.broadcast_to(im_c, (2, 256))
        for pair in range(2):
            re_p = re_c[:, pair * 128 : pair * 128 + 128]
            im_p = im_c[:, pair * 128 : pair * 128 + 128]
            even = jnp.where(low_1, re_p, pltpu.roll(im_p, CH_DEV, 1)).astype(BF16)
            odd = jnp.where(low_1, pltpu.roll(re_p, CH_DEV, 1), im_p).astype(BF16)
            folded[4 * g + 2 * pair] = even
            folded[4 * g + 2 * pair + 1] = odd
        return 0

    lax.fori_loop(0, CHANNELS // 256, fold_block, 0)

    own_copy = pltpu.make_async_copy(folded.at[chan], folded_in.at[me], own_sem)
    own_copy.start()

    def send_fold(step, _):
        other = lax.rem(me + step, DEVICES)
        pltpu.make_async_remote_copy(
            folded.at[other // N_WIN], folded_in.at[me], fold_send, fold_recv,
            device_id=place(other), device_id_type=MESH,
        ).start()
        return 0

    lax.fori_loop(1, DEVICES, send_fold, 0)
    own_copy.wait()

    low_out = lax.broadcasted_iota(jnp.int32, (128, 128), 1) < CH_DEV
    row_ids = lax.broadcasted_iota(jnp.int32, (128, 128), 0)
    lane_ids = lax.broadcasted_iota(jnp.int32, (128, 128), 1)
    mirror = jnp.where(row_ids + lane_ids == 127, 1.0, 0.0).astype(BF16)
    over_rows = (((0,), (0,)), ((), ()))

    def near(m, _):
        right = x[:, pl.ds(pl.multiple_of(m * 128, 128), 256)]
        left = jnp.dot(right[:, :128], mirror, preferred_element_type=F32)
        turned = jnp.concatenate([left[WINDOWS:], -left[:WINDOWS]], axis=0).astype(BF16)
        left = left.astype(BF16)
        re = lax.dot_general(left, right, over_rows, preferred_element_type=F32)
        im = lax.dot_general(turned, right, over_rows, preferred_element_type=F32)
        re = pltpu.roll(re, 128, 1, stride=1, stride_axis=0)[:, :128]
        im = pltpu.roll(im, 192, 1, stride=1, stride_axis=0)[:, :128]
        both = jnp.where(low_out, re, im).astype(BF16)
        for g in range(128 // ROWS):
            band[16 * m + 15 - g] = both[g * ROWS : (g + 1) * ROWS]
        return 0

    lax.fori_loop(0, N_CHAN // 2, near, 0)

    own_copy = pltpu.make_async_copy(band.at[me], band_in.at[me], own_sem)
    own_copy.start()

    def send_band(step, _):
        other = lax.rem(me + step, DEVICES)
        pltpu.make_async_remote_copy(
            band.at[other], band_in.at[me], band_send, band_recv,
            device_id=place(other), device_id_type=MESH,
        ).start()
        return 0

    lax.fori_loop(1, DEVICES, send_band, 0)
    own_copy.wait()

    inverse_copy.wait()
    spectra_copies.wait_send()
    fold_copies = all_of(folded_in, folded_in, fold_send, fold_recv)
    fold_copies.wait_send()
    fold_copies.wait_recv()
    band_copies = all_of(band, band_in, band_send, band_recv)
    band_copies.wait_send()
    band_copies.wait_recv()

    flat[...] = band_in[...].astype(F32).reshape(DEVICES * ROWS, 128)
    for r in range(ROWS):
        turned = flat[pl.ds(r, F, stride=ROWS), :].T
        at = (ROWS - 1 - r) * REACH
        lag_in[0, at : at + REACH, :] = turned[:REACH].astype(BF16)
        lag_in[1, at : at + REACH, :] = turned[REACH:].astype(BF16)
    flat_fold[...] = folded_in[...].astype(F32).reshape(DEVICES * 2, 128)
    turned_fold[...] = flat_fold[pl.ds(0, F, stride=2), :].T
    own = pl.multiple_of(win * ROWS, ROWS)
    pad = jnp.zeros((ROWS, F), F32)
    end = ROWS * REACH
    for part in range(2):
        mine = turned_fold[pl.ds(part * CH_DEV + own, ROWS), :]
        lag_in[part, end : end + 2 * ROWS, :] = jnp.concatenate([mine, pad], axis=0).astype(BF16)
    lagged = jnp.zeros((end + 2 * ROWS, NLAG), F32)
    for part in range(2):
        for half in range(2):
            lagged += jnp.dot(lag_in[part], inverse[2 * part + half], preferred_element_type=F32)
    near_ref[...] = lagged[:end].reshape(ROWS, REACH, NLAG)
    fold_ref[...] = lagged[end : end + ROWS]


def local(traces, quality, fold_block, fold_offset):
    vmem = pl.BlockSpec(memory_space=pltpu.VMEM)
    anywhere = pl.BlockSpec(memory_space=pl.ANY)
    q = jnp.tile(quality.astype(F32), GROUP)[None, :]
    idx = (fold_block[:, 0] * CH_DEV + fold_offset)[None, :]
    phases, inverse = forward_phases(), inverse_halves()
    sem = pltpu.SemaphoreType.DMA
    return pl.pallas_call(
        kernel,
        out_shape=(
            jax.ShapeDtypeStruct((ROWS, REACH, NLAG), F32),
            jax.ShapeDtypeStruct((ROWS, NLAG), F32),
        ),
        in_specs=[anywhere, vmem, vmem, anywhere, anywhere],
        out_specs=(vmem, vmem),
        scratch_shapes=[
            pltpu.VMEM((CHUNKS, LANES, L), BF16),
            pltpu.VMEM(phases.shape, F32),
            pltpu.VMEM(inverse.shape, BF16),
            pltpu.VMEM((2 * F, L), BF16),
            pltpu.VMEM((F + 16, LANES), F32),
            pltpu.VMEM((F * GROUP, 128), F32),
            pltpu.VMEM((DEVICES, CHUNKS, GROUP, 128), BF16),
            pltpu.VMEM((DEVICES, CHUNKS, GROUP, 128), BF16),
            pltpu.VMEM((2 * WINDOWS, CHANNELS + 128), BF16),
            pltpu.VMEM((CHANNELS, 256), BF16),
            pltpu.VMEM((DEVICES, ROWS, 128), BF16),
            pltpu.VMEM((N_CHAN, 2, 128), BF16),
            pltpu.VMEM((DEVICES, ROWS, 128), BF16),
            pltpu.VMEM((DEVICES, 2, 128), BF16),
            pltpu.VMEM((DEVICES * ROWS, 128), F32),
            pltpu.VMEM((DEVICES * 2, 128), F32),
            pltpu.VMEM((2, ROWS * REACH + 2 * ROWS, F), BF16),
            pltpu.VMEM((128, F), F32),
            sem((CHUNKS + 2,)),
            sem, sem, sem, sem, sem, sem, sem,
        ],
        compiler_params=pltpu.CompilerParams(
            vmem_limit_bytes=50 << 20, collective_id=0, has_side_effects=True
        ),
    )(traces.reshape(WIN_DEV * CH_DEV, L), q, idx, phases, inverse)


def solution(mesh):
    in_specs = (P("win", "chan", None), P("chan"), P(), P())
    out_specs = (P(("chan", "win"), None, None), P(("chan", "win"), None))
    return jax.shard_map(local, mesh=mesh, in_specs=in_specs, out_specs=out_specs, check_vma=False)
```

profile of v0, /device:TPU:1, one launch (start us, length us, event | category | flops | bytes accessed | tf_op | source)
XLA Modules:
  0.0 83.7 jit_solution(18388592880229804081)
XLA Ops:
  0.6 0.7 convert_element_type.3
  1.3 0.1 broadcast_in_dim_tile.3.q_ref
  1.4 0.7 broadcast_multiply_fusion
  2.1 0.7 add.3
  2.8 0.0 copy-start
  2.8 1.0 %copy-done = bf16[4,256,256]{2,1,0:T(8,128)(2,1)S(1)} copy-done((bf16[4,256,256]{2,1,0:T(8,128)(2,1)S(1)}, bf16[4,256,256]{2,1,0:T(8,128)(2,1)}, u32[]{:S(2)}) %copy-start) | copy-done | bytes 524312
  3.8 0.0 copy-start.1
  3.8 1.0 %copy-done.1 = f32[256,384]{1,0:T(8,128)S(1)} copy-done((f32[256,384]{1,0:T(8,128)S(1)}, f32[256,384]{1,0:T(8,128)}, u32[]{:S(2)}) %copy-start.1) | copy-done | bytes 393240
  4.8 77.5 %shard_map.77 = (f32[8,64,256]{2,1,0:T(8,128)S(1)}, f32[8,256]{1,0:T(8,128)S(1)}) custom-call(bf16[768,4096]{1,0:T(8,128)(2,1)} %bitcast.4, f32[1,256]{1,0:T(1,128)S(1)} %broadcast_in_dim_tile.3.q_ref, s32[1,2048]{1,0:T(1,128)S(1)} %bitcast.3, f32[256,384]{1,0:T(8,128)S(1)} %copy-done.1, bf16[4,256,256]{2,1,0:T(8,128)(2,1)S(1)} %copy-done), custom_call_target="tpu_custom_call" | custom-call | tf_op jit(solution)/shard_map/pallas_call | solution.py:281
  82.3 0.8 copy.10
  83.1 0.6 copy.11
  (1 shorter events, 0.0 us)
Async XLA Ops:
  2.8 1.0 %copy-start = (bf16[4,256,256]{2,1,0:T(8,128)(2,1)S(1)}, bf16[4,256,256]{2,1,0:T(8,128)(2,1)}, u32[]{:S(2)}) copy-start(bf16[4,256,256]{2,1,0:T(8,128)(2,1)} %constant.7.clone.inverse_hbm) | copy-start | bytes 1572868
  3.8 1.0 %copy-start.1 = (f32[256,384]{1,0:T(8,128)S(1)}, f32[256,384]{1,0:T(8,128)}, u32[]{:S(2)}) copy-start(f32[256,384]{1,0:T(8,128)} %constant.6.clone.phase_hbm) | copy-start | bytes 1179652
where the time goes:
time: 84 us; the launch traced here: 83.7 us
  Pallas kernels  77.5 us (92%)
  local copies, waits for them, and re-layouts  3.52 us (4%)
  other arithmetic  2.06 us (2%)
    pallas_call x1, Pallas kernels, local(): pl.pallas_call(kernel, out_shape=(jax.ShapeDtypeStruct((ROWS, REACH, NLAG...  77.5 us
    unnamed x6, local copies, waits for them, and re-layouts  3.43 us

commit v1 on v0

v1 whole, which is shorter than its diff:
```python
import math

import jax
import jax.numpy as jnp
import ml_dtypes
import numpy as np
from jax import lax
from jax.experimental import pallas as pl
from jax.experimental.pallas import tpu as pltpu
from jax.sharding import PartitionSpec as P

F = 256
BAND_LO = 32
NLAG = 256
REACH = 64
L = 4096
CH_DEV = 64
CHANNELS = 2048
WINDOWS = 96
N_CHAN = 32
N_WIN = 8
DEVICES = N_CHAN * N_WIN
WIN_DEV = WINDOWS // N_WIN
ROWS = CHANNELS // DEVICES
SMOOTH = 4
STEP = 128
GROUP = 4
CHUNKS = WIN_DEV // GROUP
LANES = GROUP * CH_DEV
PAIR = 2 * N_WIN
PAIRS = DEVICES // PAIR
MESH = pl.DeviceIdType.MESH
BF16 = jnp.bfloat16
F32 = jnp.float32


def forward_phases():
    frequency = np.arange(F, dtype=np.int64)[:, None] + BAND_LO
    fine = np.arange(STEP, dtype=np.int64)
    coarse = np.arange(L // STEP, dtype=np.int64) * STEP
    tables = []
    for steps in (fine, coarse):
        angles = (frequency * steps[None, :] % L).astype(np.float64) * (2.0 * math.pi / L)
        tables += [np.cos(angles), np.sin(angles)]
    joined = np.concatenate(tables, axis=1).astype(np.float32)
    return np.pad(joined, ((0, 0), (0, -joined.shape[1] % 128)))


def inverse_halves():
    shifts = np.arange(NLAG, dtype=np.int64)[None, :] + NLAG // 2
    frequency = np.arange(F, dtype=np.int64)[:, None] + BAND_LO
    angles = (frequency * shifts % NLAG).astype(np.float64) * (2.0 * math.pi / NLAG)
    factor = 1.0 / math.sqrt(F * WINDOWS)
    halves = []
    for part in (np.cos(angles) * factor, -np.sin(angles) * factor):
        high = part.astype(np.float32).astype(ml_dtypes.bfloat16)
        low = (part - high.astype(np.float64)).astype(np.float32).astype(ml_dtypes.bfloat16)
        halves += [high, low]
    return np.stack(halves)


def kernel(
    x_hbm, q_hbm, block_hbm, offset_hbm, phase_hbm, inverse_hbm, near_ref, fold_ref,
    xs, quality, fold_block, fold_offset, phase, inverse, table, energy, staged, sent, got, x, chosen,
    band, folded, band_in, folded_in, flat, flat_fold, lag_in, turned_fold,
    x_sems, in_sems, own_sem, send_sem, recv_sems, band_send, band_recv, fold_send, fold_recv,
):
    chan, win = lax.axis_index("chan"), lax.axis_index("win")
    me = chan * N_WIN + win

    def place(other):
        return (other // N_WIN, lax.rem(other, N_WIN))

    small_copies = [
        pltpu.make_async_copy(source, target, in_sems.at[i])
        for i, (source, target) in enumerate(
            [
                (phase_hbm, phase),
                (q_hbm, quality),
                (block_hbm, fold_block),
                (offset_hbm, fold_offset),
                (inverse_hbm, inverse),
            ]
        )
    ]
    x_copies = [
        pltpu.make_async_copy(x_hbm.at[pl.ds(i * LANES, LANES)], xs.at[i], x_sems.at[i])
        for i in range(CHUNKS)
    ]
    for copy in small_copies[:1] + x_copies + small_copies[1:]:
        copy.start()
    barrier = pltpu.get_barrier_semaphore()

    def greet(step, _):
        other = lax.rem(me + step, DEVICES)
        pl.semaphore_signal(barrier, inc=1, device_id=place(other), device_id_type=MESH)
        return 0

    lax.fori_loop(1, DEVICES, greet, 0)

    for copy in small_copies:
        copy.wait()
    coarse_at = 2 * STEP
    blocks = L // STEP
    fine_cos, fine_sin = phase[:, 0:STEP], phase[:, STEP : 2 * STEP]
    for block in range(blocks):
        cos_b = phase[:, coarse_at + block : coarse_at + block + 1]
        sin_b = phase[:, coarse_at + blocks + block : coarse_at + blocks + block + 1]
        lanes = slice(block * STEP, (block + 1) * STEP)
        table[0:F, lanes] = (fine_cos * cos_b - fine_sin * sin_b).astype(BF16)
        table[F : 2 * F, lanes] = (-fine_sin * cos_b - fine_cos * sin_b).astype(BF16)
    energy[0:8, :] = jnp.zeros((8, LANES), F32)
    energy[8 + F : 16 + F, :] = jnp.zeros((8, LANES), F32)

    low = lax.broadcasted_iota(jnp.int32, (F, 128), 1) < CH_DEV
    keep = jnp.concatenate([quality[...].astype(F32)] * GROUP, axis=1)
    for i in range(CHUNKS):
        x_copies[i].wait()
        spectra = lax.dot_general(
            table[...], xs[i], (((1,), (1,)), ((), ())), preferred_element_type=F32
        )
        re, im = spectra[0:F], spectra[F : 2 * F]
        power = re * re + im * im
        energy[8 : 8 + F, :] = power
        smooth = power
        for shift in range(1, SMOOTH + 1):
            smooth = smooth + (
                energy[8 - shift : 8 - shift + F, :] + energy[8 + shift : 8 + shift + F, :]
            )
        water = jnp.sum(power, axis=0, keepdims=True) * (1.0 / F)
        scaling = lax.rsqrt(smooth * (1.0 / (2 * SMOOTH + 1)) + 0.1 * water + 1e-06) * keep
        re, im = re * scaling, im * scaling
        for pair in range(GROUP // 2):
            re_p = re[:, pair * 128 : pair * 128 + 128]
            im_p = im[:, pair * 128 : pair * 128 + 128]
            first = jnp.where(low, re_p, pltpu.roll(im_p, CH_DEV, 1))
            second = jnp.where(low, pltpu.roll(re_p, CH_DEV, 1), im_p)
            staged[pl.ds(2 * pair, F, stride=GROUP), :] = first
            staged[pl.ds(2 * pair + 1, F, stride=GROUP), :] = second
        sent[:, i] = staged[...].reshape(F, GROUP, 128).astype(BF16)

    wanted_all = fold_block[...] * CH_DEV + fold_offset[...]
    fold_offset[...] = wanted_all

    def choose(g, _):
        lanes = pl.ds(pl.multiple_of(g * 256, 256), 256)
        rows = lax.broadcasted_iota(jnp.int32, (CHANNELS, 256), 0)
        chosen[:, lanes] = jnp.where(rows == fold_offset[:, lanes], 1.0, 0.0).astype(BF16)
        return 0

    lax.fori_loop(0, CHANNELS // 256, choose, 0)
    x[:, CHANNELS : CHANNELS + 128] = jnp.zeros((2 * WINDOWS, 128), BF16)

    pl.semaphore_wait(barrier, DEVICES - 1)

    pair, spot = me // PAIR, lax.rem(me, PAIR)
    own_copy = pltpu.make_async_copy(sent.at[me], got.at[me], recv_sems.at[pair])
    own_copy.start()

    def send_spectra(step, _):
        other = PAIR * lax.rem(pair + step // PAIR, PAIRS) + lax.rem(spot + step, PAIR)
        pltpu.make_async_remote_copy(
            sent.at[other], got.at[me], send_sem, recv_sems.at[pair],
            device_id=place(other), device_id_type=MESH,
        ).start()
        return 0

    lax.fori_loop(1, DEVICES, send_spectra, 0)

    def all_of(source, target, send, recv, count):
        some = pl.ds(0, count)
        return pltpu.make_async_remote_copy(
            source.at[some], target.at[some], send, recv,
            device_id=place(lax.rem(me + 1, DEVICES)), device_id_type=MESH,
        )

    low_w = lax.broadcasted_iota(jnp.int32, (WINDOWS, 128), 1) < CH_DEV
    low_out = lax.broadcasted_iota(jnp.int32, (128, 128), 1) < CH_DEV
    row_ids = lax.broadcasted_iota(jnp.int32, (128, 128), 0)
    lane_ids = lax.broadcasted_iota(jnp.int32, (128, 128), 1)
    mirror = jnp.where(row_ids + lane_ids == 127, 1.0, 0.0).astype(BF16)
    over_rows = (((0,), (0,)), ((), ()))

    def unpack(m):
        all_of(sent, got, send_sem, recv_sems.at[m], PAIR).wait_recv()
        even = got[pl.ds(PAIR * m, N_WIN)].astype(F32).reshape(WINDOWS, 128)
        odd = got[pl.ds(PAIR * m + N_WIN, N_WIN)].astype(F32).reshape(WINDOWS, 128)
        lanes = pl.ds(pl.multiple_of(m * 128, 128), 128)
        x[0:WINDOWS, lanes] = jnp.where(low_w, even, pltpu.roll(odd, CH_DEV, 1)).astype(BF16)
        x[WINDOWS : 2 * WINDOWS, lanes] = jnp.where(low_w, pltpu.roll(even, CH_DEV, 1), odd).astype(BF16)

    def near(m):
        right = x[:, pl.ds(pl.multiple_of(m * 128, 128), 256)]
        left = jnp.dot(right[:, :128], mirror, preferred_element_type=F32)
        turned = jnp.concatenate([left[WINDOWS:], -left[:WINDOWS]], axis=0).astype(BF16)
        left = left.astype(BF16)
        re = lax.dot_general(left, right, over_rows, preferred_element_type=F32)
        im = lax.dot_general(turned, right, over_rows, preferred_element_type=F32)
        re = pltpu.roll(re, 128, 1, stride=1, stride_axis=0)[:, :128]
        im = pltpu.roll(im, 192, 1, stride=1, stride_axis=0)[:, :128]
        both = jnp.where(low_out, re, im).astype(BF16)
        for g in range(PAIR):
            band[PAIR * m + PAIR - 1 - g] = both[g * ROWS : (g + 1) * ROWS]

    def send_band(m, first):
        for step in range(first, PAIR):
            other = PAIR * m + lax.rem(spot + step, PAIR)
            pltpu.make_async_remote_copy(
                band.at[other], band_in.at[me], band_send, band_recv,
                device_id=place(other), device_id_type=MESH,
            ).start()

    unpack(pair)

    def arrive(step, _):
        m = lax.rem(pair + PAIRS - step, PAIRS)
        unpack(m)
        near(m)
        send_band(m, 0)
        return 0

    lax.fori_loop(1, PAIRS, arrive, 0)
    near(pair)
    own_band = pltpu.make_async_copy(band.at[me], band_in.at[me], own_sem)
    own_band.start()
    send_band(pair, 1)

    low_1 = lax.broadcasted_iota(jnp.int32, (2, 128), 1) < CH_DEV

    def fold_group(g, _):
        lanes = pl.ds(pl.multiple_of(g * 256, 256), 256)
        partner = jnp.dot(x[:, 0:CHANNELS], chosen[:, lanes], preferred_element_type=F32)
        own = x[:, lanes].astype(F32)
        re_a, im_a = own[:WINDOWS], own[WINDOWS:]
        re_b, im_b = partner[:WINDOWS], partner[WINDOWS:]
        re_c = jnp.sum(re_a * re_b + im_a * im_b, axis=0, keepdims=True)
        im_c = jnp.sum(im_a * re_b - re_a * im_b, axis=0, keepdims=True)
        re_c = jnp.broadcast_to(re_c, (2, 256))
        im_c = jnp.broadcast_to(im_c, (2, 256))
        for half in range(2):
            re_p = re_c[:, half * 128 : half * 128 + 128]
            im_p = im_c[:, half * 128 : half * 128 + 128]
            even = jnp.where(low_1, re_p, pltpu.roll(im_p, CH_DEV, 1)).astype(BF16)
            odd = jnp.where(low_1, pltpu.roll(re_p, CH_DEV, 1), im_p).astype(BF16)
            folded[4 * g + 2 * half] = even
            folded[4 * g + 2 * half + 1] = odd
        return 0

    lax.fori_loop(0, CHANNELS // 256, fold_group, 0)

    own_band.wait()
    own_fold = pltpu.make_async_copy(folded.at[chan], folded_in.at[me], own_sem)
    own_fold.start()

    def send_fold(step, _):
        other = lax.rem(me + step, DEVICES)
        pltpu.make_async_remote_copy(
            folded.at[other // N_WIN], folded_in.at[me], fold_send, fold_recv,
            device_id=place(other), device_id_type=MESH,
        ).start()
        return 0

    lax.fori_loop(1, DEVICES, send_fold, 0)
    own_fold.wait()

    all_of(sent, got, send_sem, recv_sems.at[0], DEVICES - 1).wait_send()
    band_copies = all_of(band, band_in, band_send, band_recv, DEVICES - 1)
    band_copies.wait_send()
    band_copies.wait_recv()
    fold_copies = all_of(folded_in, folded_in, fold_send, fold_recv, DEVICES - 1)
    fold_copies.wait_send()
    fold_copies.wait_recv()

    flat[...] = band_in[...].astype(F32).reshape(DEVICES * ROWS, 128)
    for r in range(ROWS):
        turned = flat[pl.ds(r, F, stride=ROWS), :].T
        at = (ROWS - 1 - r) * REACH
        lag_in[0, at : at + REACH, :] = turned[:REACH].astype(BF16)
        lag_in[1, at : at + REACH, :] = turned[REACH:].astype(BF16)
    flat_fold[...] = folded_in[...].astype(F32).reshape(DEVICES * 2, 128)
    turned_fold[...] = flat_fold[pl.ds(0, F, stride=2), :].T
    own = pl.multiple_of(win * ROWS, ROWS)
    pad = jnp.zeros((ROWS, F), F32)
    end = ROWS * REACH
    for part in range(2):
        mine = turned_fold[pl.ds(part * CH_DEV + own, ROWS), :]
        lag_in[part, end : end + 2 * ROWS, :] = jnp.concatenate([mine, pad], axis=0).astype(BF16)
    lagged = jnp.zeros((end + 2 * ROWS, NLAG), F32)
    for part in range(2):
        for half in range(2):
            lagged += jnp.dot(lag_in[part], inverse[2 * part + half], preferred_element_type=F32)
    near_ref[...] = lagged[:end].reshape(ROWS, REACH, NLAG)
    fold_ref[...] = lagged[end : end + ROWS]


def local(traces, quality, fold_block, fold_offset):
    vmem = pl.BlockSpec(memory_space=pltpu.VMEM)
    hbm = pl.BlockSpec(memory_space=pltpu.MemorySpace.HBM)
    phases, inverse = forward_phases(), inverse_halves()
    sem = pltpu.SemaphoreType.DMA
    return pl.pallas_call(
        kernel,
        out_shape=(
            jax.ShapeDtypeStruct((ROWS, REACH, NLAG), F32),
            jax.ShapeDtypeStruct((ROWS, NLAG), F32),
        ),
        in_specs=[hbm] * 6,
        out_specs=(vmem, vmem),
        scratch_shapes=[
            pltpu.VMEM((CHUNKS, LANES, L), BF16),
            pltpu.VMEM((1, CH_DEV), jnp.int32),
            pltpu.VMEM((1, CHANNELS), jnp.int32),
            pltpu.VMEM((1, CHANNELS), jnp.int32),
            pltpu.VMEM(phases.shape, F32),
            pltpu.VMEM(inverse.shape, BF16),
            pltpu.VMEM((2 * F, L), BF16),
            pltpu.VMEM((F + 16, LANES), F32),
            pltpu.VMEM((F * GROUP, 128), F32),
            pltpu.VMEM((DEVICES, CHUNKS, GROUP, 128), BF16),
            pltpu.VMEM((DEVICES, CHUNKS, GROUP, 128), BF16),
            pltpu.VMEM((2 * WINDOWS, CHANNELS + 128), BF16),
            pltpu.VMEM((CHANNELS, CHANNELS), BF16),
            pltpu.VMEM((DEVICES, ROWS, 128), BF16),
            pltpu.VMEM((N_CHAN, 2, 128), BF16),
            pltpu.VMEM((DEVICES, ROWS, 128), BF16),
            pltpu.VMEM((DEVICES, 2, 128), BF16),
            pltpu.VMEM((DEVICES * ROWS, 128), F32),
            pltpu.VMEM((DEVICES * 2, 128), F32),
            pltpu.VMEM((2, ROWS * REACH + 2 * ROWS, F), BF16),
            pltpu.VMEM((128, F), F32),
            sem((CHUNKS,)),
            sem((5,)),
            sem,
            sem,
            sem((PAIRS,)),
            sem, sem, sem, sem,
        ],
        compiler_params=pltpu.CompilerParams(
            vmem_limit_bytes=63 << 20, collective_id=0, has_side_effects=True
        ),
    )(
        traces.reshape(WIN_DEV * CH_DEV, L),
        quality.reshape(1, CH_DEV),
        fold_block.reshape(1, CHANNELS),
        fold_offset.reshape(1, CHANNELS),
        phases,
        inverse,
    )


def solution(mesh):
    in_specs = (P("win", "chan", None), P("chan"), P(), P())
    out_specs = (P(("chan", "win"), None, None), P(("chan", "win"), None))
    return jax.shard_map(local, mesh=mesh, in_specs=in_specs, out_specs=out_specs, check_vma=False)
```

time: 84 us -> 71.6 us (0.85)
  Pallas kernels: 77.5 us -> 67.6 us
  other arithmetic: 2.06 us -> 0 us
    pallas_call x1, Pallas kernels: 77.5 us -> 67.6 us  [local(): pl.pallas_call(kernel, out_shape=(jax.ShapeDtypeStruct((ROWS, REACH, NLAG...]
    unnamed x6 -> x2, local copies, waits for them, and re-layouts: 3.43 us -> 3.16 us
where the time goes in v1:
time: 71.6 us; the launch traced here: 71.4 us
  Pallas kernels  67.6 us (94%)
  local copies, waits for them, and re-layouts  3.16 us (4%)
    pallas_call x1, Pallas kernels, local(): pl.pallas_call(kernel, out_shape=(jax.ShapeDtypeStruct((ROWS, REACH, NLAG...  67.6 us
    unnamed x2, local copies, waits for them, and re-layouts  3.16 us

profile of v1, /device:TPU:1, one launch (start us, length us, event | category | flops | bytes accessed | tf_op | source)
XLA Modules:
  0.0 71.4 jit_solution(13280005907180949640)
XLA Ops:
  0.6 67.6 %shard_map.77 = (f32[8,64,256]{2,1,0:T(8,128)}, f32[8,256]{1,0:T(8,128)}) custom-call(bf16[768,4096]{1,0:T(8,128)(2,1)} %bitcast.4, s32[1,64]{1,0:T(1,128)} %bitcast.7, s32[1,2048]{1,0:T(1,128)} %bitcast.5, s32[1,2048]{1,0:T(1,128)} %bitcast.6, f32[256,384]{1,0:T(8,128)} %constant.4.clone.phase_hbm, bf16[4,256,256]{2,1,0:T(8,128)(2,1)} %constant.5.clone.inverse_hbm), custom_call_target="tpu_custom_call" | custom-call | tf_op jit(solution)/shard_map/pallas_call | solution.py:301
  68.2 1.9 %copy.10 = f32[8,64,256]{2,1,0:T(8,128)} copy(f32[8,64,256]{2,1,0:T(8,128)} %get-tuple-element.4) | data formatting | bytes 1048576
  70.1 1.3 %copy.11 = f32[8,256]{1,0:T(8,128)} copy(f32[8,256]{1,0:T(8,128)} %get-tuple-element.5) | data formatting | bytes 16384

commit v2 on v1

--- a/solution.py
+++ b/solution.py
@@ -29,6 +29,7 @@
 LANES = GROUP * CH_DEV
 PAIR = 2 * N_WIN
 PAIRS = DEVICES // PAIR
+GREETED = 96
 MESH = pl.DeviceIdType.MESH
 BF16 = jnp.bfloat16
 F32 = jnp.float32
@@ -62,8 +63,8 @@
 def kernel(
     x_hbm, q_hbm, block_hbm, offset_hbm, phase_hbm, inverse_hbm, near_ref, fold_ref,
     xs, quality, fold_block, fold_offset, phase, inverse, table, energy, staged, sent, got, x, chosen,
-    band, folded, band_in, folded_in, flat, flat_fold, lag_in, turned_fold,
-    x_sems, in_sems, own_sem, send_sem, recv_sems, band_send, band_recv, fold_send, fold_recv,
+    band, folded, band_in, folded_in, flat, flat_fold, by_bin, lag_in, turned_fold,
+    x_sems, in_sems, own_sems, send_sem, recv_sems, band_send, band_recv, fold_send, fold_recv, relay_send, relay_recv,
 ):
     chan, win = lax.axis_index("chan"), lax.axis_index("win")
     me = chan * N_WIN + win
@@ -87,7 +88,7 @@
         pltpu.make_async_copy(x_hbm.at[pl.ds(i * LANES, LANES)], xs.at[i], x_sems.at[i])
         for i in range(CHUNKS)
     ]
-    for copy in small_copies[:1] + x_copies + small_copies[1:]:
+    for copy in small_copies[:4] + x_copies + small_copies[4:]:
         copy.start()
     barrier = pltpu.get_barrier_semaphore()
 
@@ -96,10 +97,9 @@
         pl.semaphore_signal(barrier, inc=1, device_id=place(other), device_id_type=MESH)
         return 0
 
-    lax.fori_loop(1, DEVICES, greet, 0)
-
-    for copy in small_copies:
-        copy.wait()
+    lax.fori_loop(1, GREETED, greet, 0)
+
+    small_copies[0].wait()
     coarse_at = 2 * STEP
     blocks = L // STEP
     fine_cos, fine_sin = phase[:, 0:STEP], phase[:, STEP : 2 * STEP]
@@ -109,9 +109,13 @@
         lanes = slice(block * STEP, (block + 1) * STEP)
         table[0:F, lanes] = (fine_cos * cos_b - fine_sin * sin_b).astype(BF16)
         table[F : 2 * F, lanes] = (-fine_sin * cos_b - fine_cos * sin_b).astype(BF16)
+        for step in range(GREETED + block, DEVICES, blocks):
+            greet(step, 0)
     energy[0:8, :] = jnp.zeros((8, LANES), F32)
     energy[8 + F : 16 + F, :] = jnp.zeros((8, LANES), F32)
 
+    for copy in small_copies[1:4]:
+        copy.wait()
     low = lax.broadcasted_iota(jnp.int32, (F, 128), 1) < CH_DEV
     keep = jnp.concatenate([quality[...].astype(F32)] * GROUP, axis=1)
     for i in range(CHUNKS):
@@ -139,18 +143,6 @@
             staged[pl.ds(2 * pair + 1, F, stride=GROUP), :] = second
         sent[:, i] = staged[...].reshape(F, GROUP, 128).astype(BF16)
 
-    wanted_all = fold_block[...] * CH_DEV + fold_offset[...]
-    fold_offset[...] = wanted_all
-
-    def choose(g, _):
-        lanes = pl.ds(pl.multiple_of(g * 256, 256), 256)
-        rows = lax.broadcasted_iota(jnp.int32, (CHANNELS, 256), 0)
-        chosen[:, lanes] = jnp.where(rows == fold_offset[:, lanes], 1.0, 0.0).astype(BF16)
-        return 0
-
-    lax.fori_loop(0, CHANNELS // 256, choose, 0)
-    x[:, CHANNELS : CHANNELS + 128] = jnp.zeros((2 * WINDOWS, 128), BF16)
-
     pl.semaphore_wait(barrier, DEVICES - 1)
 
     pair, spot = me // PAIR, lax.rem(me, PAIR)
@@ -166,6 +158,18 @@
         return 0
 
     lax.fori_loop(1, DEVICES, send_spectra, 0)
+
+    wanted_all = fold_block[...] * CH_DEV + fold_offset[...]
+    fold_offset[...] = wanted_all
+
+    def choose(g, _):
+        lanes = pl.ds(pl.multiple_of(g * 256, 256), 256)
+        rows = lax.broadcasted_iota(jnp.int32, (CHANNELS, 256), 0)
+        chosen[:, lanes] = jnp.where(rows == fold_offset[:, lanes], 1.0, 0.0).astype(BF16)
+        return 0
+
+    lax.fori_loop(0, CHANNELS // 256, choose, 0)
+    x[:, CHANNELS : CHANNELS + 128] = jnp.zeros((2 * WINDOWS, 128), BF16)
 
     def all_of(source, target, send, recv, count):
         some = pl.ds(0, count)
@@ -219,11 +223,9 @@
         send_band(m, 0)
         return 0
 
-    lax.fori_loop(1, PAIRS, arrive, 0)
-    near(pair)
-    own_band = pltpu.make_async_copy(band.at[me], band_in.at[me], own_sem)
-    own_band.start()
-    send_band(pair, 1)
+    lax.fori_loop(1, PAIRS - 1, arrive, 0)
+    last = lax.rem(pair + 1, PAIRS)
+    unpack(last)
 
     low_1 = lax.broadcasted_iota(jnp.int32, (2, 128), 1) < CH_DEV
 
@@ -248,28 +250,49 @@
 
     lax.fori_loop(0, CHANNELS // 256, fold_group, 0)
 
-    own_band.wait()
-    own_fold = pltpu.make_async_copy(folded.at[chan], folded_in.at[me], own_sem)
+    own_fold = pltpu.make_async_copy(folded.at[chan], folded_in.at[win, chan], own_sems.at[0])
     own_fold.start()
 
     def send_fold(step, _):
-        other = lax.rem(me + step, DEVICES)
+        other = lax.rem(chan + step, N_CHAN)
         pltpu.make_async_remote_copy(
-            folded.at[other // N_WIN], folded_in.at[me], fold_send, fold_recv,
-            device_id=place(other), device_id_type=MESH,
+            folded.at[other], folded_in.at[win, chan], fold_send, fold_recv,
+            device_id=(other, win), device_id_type=MESH,
         ).start()
         return 0
 
-    lax.fori_loop(1, DEVICES, send_fold, 0)
+    lax.fori_loop(1, N_CHAN, send_fold, 0)
+
+    near(last)
+    send_band(last, 0)
+    near(pair)
+    own_band = pltpu.make_async_copy(band.at[me], band_in.at[me], own_sems.at[1])
+    own_band.start()
+    send_band(pair, 1)
+
     own_fold.wait()
+    fold_copies = all_of(folded, folded, fold_send, fold_recv, N_CHAN - 1)
+    fold_copies.wait_recv()
+
+    def relay(step, _):
+        pltpu.make_async_remote_copy(
+            folded_in.at[win], folded_in.at[win], relay_send, relay_recv,
+            device_id=(chan, lax.rem(win + step, N_WIN)), device_id_type=MESH,
+        ).start()
+        return 0
+
+    lax.fori_loop(1, N_WIN, relay, 0)
 
     all_of(sent, got, send_sem, recv_sems.at[0], DEVICES - 1).wait_send()
     band_copies = all_of(band, band_in, band_send, band_recv, DEVICES - 1)
     band_copies.wait_send()
     band_copies.wait_recv()
-    fold_copies = all_of(folded_in, folded_in, fold_send, fold_recv, DEVICES - 1)
     fold_copies.wait_send()
-    fold_copies.wait_recv()
+    relay_copies = all_of(folded_in, folded_in, relay_send, relay_recv, N_WIN - 1)
+    relay_copies.wait_send()
+    relay_copies.wait_recv()
+    own_band.wait()
+    small_copies[4].wait()
 
     flat[...] = band_in[...].astype(F32).reshape(DEVICES * ROWS, 128)
     for r in range(ROWS):
@@ -278,7 +301,10 @@
         lag_in[0, at : at + REACH, :] = turned[:REACH].astype(BF16)
         lag_in[1, at : at + REACH, :] = turned[REACH:].astype(BF16)
     flat_fold[...] = folded_in[...].astype(F32).reshape(DEVICES * 2, 128)
-    turned_fold[...] = flat_fold[pl.ds(0, F, stride=2), :].T
+    for w in range(N_WIN):
+        rows = flat_fold[pl.ds(2 * N_CHAN * w, N_CHAN, stride=2), :]
+        by_bin[pl.ds(w, N_CHAN, stride=N_WIN), :] = rows
+    turned_fold[...] = by_bin[...].T
     own = pl.multiple_of(win * ROWS, ROWS)
     pad = jnp.zeros((ROWS, F), F32)
     end = ROWS * REACH
@@ -323,20 +349,21 @@
             pltpu.VMEM((DEVICES, ROWS, 128), BF16),
             pltpu.VMEM((N_CHAN, 2, 128), BF16),
             pltpu.VMEM((DEVICES, ROWS, 128), BF16),
-            pltpu.VMEM((DEVICES, 2, 128), BF16),
+            pltpu.VMEM((N_WIN, N_CHAN, 2, 128), BF16),
             pltpu.VMEM((DEVICES * ROWS, 128), F32),
             pltpu.VMEM((DEVICES * 2, 128), F32),
+            pltpu.VMEM((F, 128), F32),
             pltpu.VMEM((2, ROWS * REACH + 2 * ROWS, F), BF16),
             pltpu.VMEM((128, F), F32),
             sem((CHUNKS,)),
             sem((5,)),
-            sem,
+            sem((2,)),
             sem,
             sem((PAIRS,)),
-            sem, sem, sem, sem,
+            sem, sem, sem, sem, sem, sem,
         ],
         compiler_params=pltpu.CompilerParams(
-            vmem_limit_bytes=63 << 20, collective_id=0, has_side_effects=True
+            vmem_limit_bytes=60 << 20, collective_id=0, has_side_effects=True
         ),
     )(
         traces.reshape(WIN_DEV * CH_DEV, L),

time: 71.6 us -> 67.5 us (0.943)
  Pallas kernels: 67.6 us -> 63.6 us
    pallas_call x1, Pallas kernels: 67.6 us -> 63.6 us  [local(): pl.pallas_call(kernel, out_shape=(jax.ShapeDtypeStruct((ROWS, REACH, NLAG...]
where the time goes in v2:
time: 67.5 us; the launch traced here: 67.4 us
  Pallas kernels  63.6 us (94%)
  local copies, waits for them, and re-layouts  3.16 us (5%)
    pallas_call x1, Pallas kernels, local(): pl.pallas_call(kernel, out_shape=(jax.ShapeDtypeStruct((ROWS, REACH, NLAG...  63.6 us
    unnamed x2, local copies, waits for them, and re-layouts  3.16 us

profile of v2, /device:TPU:1, one launch (start us, length us, event | category | flops | bytes accessed | tf_op | source)
XLA Modules:
  0.0 67.4 jit_solution(8809283923844355628)
XLA Ops:
  0.6 63.6 %shard_map.77 = (f32[8,64,256]{2,1,0:T(8,128)}, f32[8,256]{1,0:T(8,128)}) custom-call(bf16[768,4096]{1,0:T(8,128)(2,1)} %bitcast.4, s32[1,64]{1,0:T(1,128)} %bitcast.7, s32[1,2048]{1,0:T(1,128)} %bitcast.5, s32[1,2048]{1,0:T(1,128)} %bitcast.6, f32[256,384]{1,0:T(8,128)} %constant.4.clone.phase_hbm, bf16[4,256,256]{2,1,0:T(8,128)(2,1)} %constant.5.clone.inverse_hbm), custom_call_target="tpu_custom_call" | custom-call | tf_op jit(solution)/shard_map/pallas_call | solution.py:327
  64.2 1.9 %copy.10 = f32[8,64,256]{2,1,0:T(8,128)} copy(f32[8,64,256]{2,1,0:T(8,128)} %get-tuple-element.4) | data formatting | bytes 1048576
  66.1 1.3 %copy.11 = f32[8,256]{1,0:T(8,128)} copy(f32[8,256]{1,0:T(8,128)} %get-tuple-element.5) | data formatting | bytes 16384

commit v3 on v2

--- a/solution.py
+++ b/solution.py
@@ -29,7 +29,7 @@
 LANES = GROUP * CH_DEV
 PAIR = 2 * N_WIN
 PAIRS = DEVICES // PAIR
-GREETED = 96
+GREETED = 13
 MESH = pl.DeviceIdType.MESH
 BF16 = jnp.bfloat16
 F32 = jnp.float32
@@ -51,9 +51,8 @@
     shifts = np.arange(NLAG, dtype=np.int64)[None, :] + NLAG // 2
     frequency = np.arange(F, dtype=np.int64)[:, None] + BAND_LO
     angles = (frequency * shifts % NLAG).astype(np.float64) * (2.0 * math.pi / NLAG)
-    factor = 1.0 / math.sqrt(F * WINDOWS)
     halves = []
-    for part in (np.cos(angles) * factor, -np.sin(angles) * factor):
+    for part in (np.cos(angles), -np.sin(angles)):
         high = part.astype(np.float32).astype(ml_dtypes.bfloat16)
         low = (part - high.astype(np.float64)).astype(np.float32).astype(ml_dtypes.bfloat16)
         halves += [high, low]
@@ -69,8 +68,10 @@
     chan, win = lax.axis_index("chan"), lax.axis_index("win")
     me = chan * N_WIN + win
 
-    def place(other):
-        return (other // N_WIN, lax.rem(other, N_WIN))
+    wins = [lax.rem(win + k, N_WIN) for k in range(N_WIN)]
+    side = lax.rem(chan, 2)
+    sides = (side, 1 - side)
+    neighbour = (lax.rem(chan + 1, N_CHAN), win)
 
     small_copies = [
         pltpu.make_async_copy(source, target, in_sems.at[i])
@@ -93,10 +94,13 @@
     barrier = pltpu.get_barrier_semaphore()
 
     def greet(step, _):
-        other = lax.rem(me + step, DEVICES)
-        pl.semaphore_signal(barrier, inc=1, device_id=place(other), device_id_type=MESH)
-        return 0
-
+        other = lax.rem(chan + step, N_CHAN)
+        for k in range(N_WIN):
+            pl.semaphore_signal(barrier, inc=1, device_id=(other, wins[k]), device_id_type=MESH)
+        return 0
+
+    for k in range(1, N_WIN):
+        pl.semaphore_signal(barrier, inc=1, device_id=(chan, wins[k]), device_id_type=MESH)
     lax.fori_loop(1, GREETED, greet, 0)
 
     small_copies[0].wait()
@@ -109,8 +113,8 @@
         lanes = slice(block * STEP, (block + 1) * STEP)
         table[0:F, lanes] = (fine_cos * cos_b - fine_sin * sin_b).astype(BF16)
         table[F : 2 * F, lanes] = (-fine_sin * cos_b - fine_cos * sin_b).astype(BF16)
-        for step in range(GREETED + block, DEVICES, blocks):
-            greet(step, 0)
+        if GREETED <= block < N_CHAN:
+            greet(block, 0)
     energy[0:8, :] = jnp.zeros((8, LANES), F32)
     energy[8 + F : 16 + F, :] = jnp.zeros((8, LANES), F32)
 
@@ -145,19 +149,26 @@
 
     pl.semaphore_wait(barrier, DEVICES - 1)
 
-    pair, spot = me // PAIR, lax.rem(me, PAIR)
+    pair = chan // 2
     own_copy = pltpu.make_async_copy(sent.at[me], got.at[me], recv_sems.at[pair])
     own_copy.start()
 
+    def send_to(source, target, send, recv, m, own):
+        for h in range(2):
+            other = 2 * m + sides[h]
+            for k in range(1 if own and h == 0 else 0, N_WIN):
+                pltpu.make_async_remote_copy(
+                    source.at[other * N_WIN + wins[k]], target.at[me], send, recv,
+                    device_id=(other, wins[k]), device_id_type=MESH,
+                ).start()
+
     def send_spectra(step, _):
-        other = PAIR * lax.rem(pair + step // PAIR, PAIRS) + lax.rem(spot + step, PAIR)
-        pltpu.make_async_remote_copy(
-            sent.at[other], got.at[me], send_sem, recv_sems.at[pair],
-            device_id=place(other), device_id_type=MESH,
-        ).start()
-        return 0
-
-    lax.fori_loop(1, DEVICES, send_spectra, 0)
+        m = lax.rem(pair + step, PAIRS)
+        send_to(sent, got, send_sem, recv_sems.at[pair], m, False)
+        return 0
+
+    send_to(sent, got, send_sem, recv_sems.at[pair], pair, True)
+    lax.fori_loop(1, PAIRS, send_spectra, 0)
 
     wanted_all = fold_block[...] * CH_DEV + fold_offset[...]
     fold_offset[...] = wanted_all
@@ -175,7 +186,7 @@
         some = pl.ds(0, count)
         return pltpu.make_async_remote_copy(
             source.at[some], target.at[some], send, recv,
-            device_id=place(lax.rem(me + 1, DEVICES)), device_id_type=MESH,
+            device_id=neighbour, device_id_type=MESH,
         )
 
     low_w = lax.broadcasted_iota(jnp.int32, (WINDOWS, 128), 1) < CH_DEV
@@ -206,13 +217,8 @@
         for g in range(PAIR):
             band[PAIR * m + PAIR - 1 - g] = both[g * ROWS : (g + 1) * ROWS]
 
-    def send_band(m, first):
-        for step in range(first, PAIR):
-            other = PAIR * m + lax.rem(spot + step, PAIR)
-            pltpu.make_async_remote_copy(
-                band.at[other], band_in.at[me], band_send, band_recv,
-                device_id=place(other), device_id_type=MESH,
-            ).start()
+    def send_band(m, own):
+        send_to(band, band_in, band_send, band_recv, m, own)
 
     unpack(pair)
 
@@ -220,7 +226,7 @@
         m = lax.rem(pair + PAIRS - step, PAIRS)
         unpack(m)
         near(m)
-        send_band(m, 0)
+        send_band(m, False)
         return 0
 
     lax.fori_loop(1, PAIRS - 1, arrive, 0)
@@ -264,11 +270,11 @@
     lax.fori_loop(1, N_CHAN, send_fold, 0)
 
     near(last)
-    send_band(last, 0)
+    send_band(last, False)
     near(pair)
     own_band = pltpu.make_async_copy(band.at[me], band_in.at[me], own_sems.at[1])
     own_band.start()
-    send_band(pair, 1)
+    send_band(pair, True)
 
     own_fold.wait()
     fold_copies = all_of(folded, folded, fold_send, fold_recv, N_CHAN - 1)
@@ -324,7 +330,7 @@
     hbm = pl.BlockSpec(memory_space=pltpu.MemorySpace.HBM)
     phases, inverse = forward_phases(), inverse_halves()
     sem = pltpu.SemaphoreType.DMA
-    return pl.pallas_call(
+    near_lags, fold_lags = pl.pallas_call(
         kernel,
         out_shape=(
             jax.ShapeDtypeStruct((ROWS, REACH, NLAG), F32),
@@ -373,6 +379,8 @@
         phases,
         inverse,
     )
+    factor = 1.0 / math.sqrt(F * WINDOWS)
+    return near_lags * factor, fold_lags * factor
 
 
 def solution(mesh):

time: 67.5 us -> 64.1 us (0.950)
  Pallas kernels: 63.6 us -> 60.1 us
  other arithmetic: 0 us -> 3.18 us
  local copies, waits for them, and re-layouts: 3.16 us -> 0 us
    pallas_call x1, Pallas kernels: 63.6 us -> 60.1 us  [local(): pl.pallas_call(kernel, out_shape=(jax.ShapeDtypeStruct((ROWS, REACH, NLAG...]
    mul x0 -> x2, other arithmetic: none -> 3.18 us  [local(): return (near_lags * factor, fold_lags * factor)]
    unnamed x2 -> x0, local copies, waits for them, and re-layouts: 3.16 us -> none
where the time goes in v3:
time: 64.1 us; the launch traced here: 63.9 us
  Pallas kernels  60.1 us (94%)
  other arithmetic  3.18 us (5%)
    pallas_call x1, Pallas kernels, local(): pl.pallas_call(kernel, out_shape=(jax.ShapeDtypeStruct((ROWS, REACH, NLAG...  60.1 us
    mul x2, other arithmetic, local(): return (near_lags * factor, fold_lags * factor)  3.18 us

profile of v3, /device:TPU:1, one launch (start us, length us, event | category | flops | bytes accessed | tf_op | source)
XLA Modules:
  0.0 63.9 jit_solution(10669215834937407631)
XLA Ops:
  0.6 60.1 %shard_map.77 = (f32[8,64,256]{2,1,0:T(8,128)}, f32[8,256]{1,0:T(8,128)}) custom-call(bf16[768,4096]{1,0:T(8,128)(2,1)} %bitcast.4, s32[1,64]{1,0:T(1,128)} %bitcast.7, s32[1,2048]{1,0:T(1,128)} %bitcast.5, s32[1,2048]{1,0:T(1,128)} %bitcast.6, f32[256,384]{1,0:T(8,128)} %constant.2.clone.phase_hbm, bf16[4,256,256]{2,1,0:T(8,128)(2,1)} %constant.8.clone.inverse_hbm), custom_call_target="tpu_custom_call" | custom-call | tf_op jit(solution)/shard_map/pallas_call | solution.py:333
  60.7 1.9 %broadcast_multiply_fusion = f32[8,64,256]{2,1,0:T(8,128)} fusion(f32[8,64,256]{2,1,0:T(8,128)} %get-tuple-element.4), kind=kLoop, calls=%fused_computation | loop fusion | flops 131072 | bytes 1048576 | tf_op jit(solution)/shard_map/mul | solution.py:383
  62.6 1.3 %broadcast_multiply_fusion.1 = f32[8,256]{1,0:T(8,128)} fusion(f32[8,256]{1,0:T(8,128)} %get-tuple-element.5), kind=kLoop, calls=%fused_computation.1 | loop fusion | flops 2048 | bytes 16384 | tf_op jit(solution)/shard_map/mul | solution.py:383

commit v4 on v3

--- a/solution.py
+++ b/solution.py
@@ -29,6 +29,7 @@
 LANES = GROUP * CH_DEV
 PAIR = 2 * N_WIN
 PAIRS = DEVICES // PAIR
+HALF = F // 2
 GREETED = 13
 MESH = pl.DeviceIdType.MESH
 BF16 = jnp.bfloat16
@@ -36,9 +37,10 @@
 
 
 def forward_phases():
-    frequency = np.arange(F, dtype=np.int64)[:, None] + BAND_LO
+    bins = np.arange(F, dtype=np.int64).reshape(HALF, 2).T.reshape(F)
+    frequency = bins[:, None] + BAND_LO
     fine = np.arange(STEP, dtype=np.int64)
-    coarse = np.arange(L // STEP, dtype=np.int64) * STEP
+    coarse = np.arange(L // 2 // STEP, dtype=np.int64) * STEP
     tables = []
     for steps in (fine, coarse):
         angles = (frequency * steps[None, :] % L).astype(np.float64) * (2.0 * math.pi / L)
@@ -105,46 +107,59 @@
 
     small_copies[0].wait()
     coarse_at = 2 * STEP
-    blocks = L // STEP
+    blocks = L // 2 // STEP
     fine_cos, fine_sin = phase[:, 0:STEP], phase[:, STEP : 2 * STEP]
-    for block in range(blocks):
+    for block in range(max(blocks, N_CHAN)):
+        if GREETED <= block < N_CHAN:
+            greet(block, 0)
+        if block >= blocks:
+            continue
         cos_b = phase[:, coarse_at + block : coarse_at + block + 1]
         sin_b = phase[:, coarse_at + blocks + block : coarse_at + blocks + block + 1]
         lanes = slice(block * STEP, (block + 1) * STEP)
-        table[0:F, lanes] = (fine_cos * cos_b - fine_sin * sin_b).astype(BF16)
-        table[F : 2 * F, lanes] = (-fine_sin * cos_b - fine_cos * sin_b).astype(BF16)
-        if GREETED <= block < N_CHAN:
-            greet(block, 0)
-    energy[0:8, :] = jnp.zeros((8, LANES), F32)
-    energy[8 + F : 16 + F, :] = jnp.zeros((8, LANES), F32)
+        cosines = (fine_cos * cos_b - fine_sin * sin_b).astype(BF16)
+        sines = (-fine_sin * cos_b - fine_cos * sin_b).astype(BF16)
+        for odd in range(2):
+            table[odd, 0:HALF, lanes] = cosines[odd * HALF : (odd + 1) * HALF]
+            table[odd, HALF:F, lanes] = sines[odd * HALF : (odd + 1) * HALF]
+    edge = jnp.zeros((8, LANES), F32)
+    for odd in range(2):
+        energy[odd, 0:8, :] = edge
+        energy[odd, 8 + HALF : 16 + HALF, :] = edge
 
     for copy in small_copies[1:4]:
         copy.wait()
-    low = lax.broadcasted_iota(jnp.int32, (F, 128), 1) < CH_DEV
+    low = lax.broadcasted_iota(jnp.int32, (HALF, 128), 1) < CH_DEV
     keep = jnp.concatenate([quality[...].astype(F32)] * GROUP, axis=1)
+    over_lanes = (((1,), (1,)), ((), ()))
     for i in range(CHUNKS):
         x_copies[i].wait()
-        spectra = lax.dot_general(
-            table[...], xs[i], (((1,), (1,)), ((), ())), preferred_element_type=F32
-        )
-        re, im = spectra[0:F], spectra[F : 2 * F]
-        power = re * re + im * im
-        energy[8 : 8 + F, :] = power
-        smooth = power
-        for shift in range(1, SMOOTH + 1):
-            smooth = smooth + (
-                energy[8 - shift : 8 - shift + F, :] + energy[8 + shift : 8 + shift + F, :]
-            )
-        water = jnp.sum(power, axis=0, keepdims=True) * (1.0 / F)
-        scaling = lax.rsqrt(smooth * (1.0 / (2 * SMOOTH + 1)) + 0.1 * water + 1e-06) * keep
-        re, im = re * scaling, im * scaling
-        for pair in range(GROUP // 2):
-            re_p = re[:, pair * 128 : pair * 128 + 128]
-            im_p = im[:, pair * 128 : pair * 128 + 128]
-            first = jnp.where(low, re_p, pltpu.roll(im_p, CH_DEV, 1))
-            second = jnp.where(low, pltpu.roll(re_p, CH_DEV, 1), im_p)
-            staged[pl.ds(2 * pair, F, stride=GROUP), :] = first
-            staged[pl.ds(2 * pair + 1, F, stride=GROUP), :] = second
+        early, late = xs[i, :, 0 : L // 2], xs[i, :, L // 2 : L]
+        parts, powers = [], []
+        for odd, mixed in enumerate((early + late, early - late)):
+            spectra = lax.dot_general(table[odd], mixed, over_lanes, preferred_element_type=F32)
+            re, im = spectra[0:HALF], spectra[HALF:F]
+            power = re * re + im * im
+            energy[odd, 8 : 8 + HALF, :] = power
+            parts.append((re, im))
+            powers.append(power)
+        water = jnp.sum(powers[0] + powers[1], axis=0, keepdims=True) * (1.0 / F)
+        for odd, (re, im) in enumerate(parts):
+            near_bins = [(odd, d) for d in (-2, -1, 1, 2)]
+            near_bins += [(1 - odd, d) for d in ((-1, 0, 1, 2) if odd else (-2, -1, 0, 1))]
+            smooth = powers[odd]
+            for which, d in near_bins:
+                smooth = smooth + energy[which, 8 + d : 8 + d + HALF, :]
+            scaling = lax.rsqrt(smooth * (1.0 / (2 * SMOOTH + 1)) + 0.1 * water + 1e-06) * keep
+            re, im = re * scaling, im * scaling
+            for half in range(GROUP // 2):
+                re_p = re[:, half * 128 : half * 128 + 128]
+                im_p = im[:, half * 128 : half * 128 + 128]
+                first = jnp.where(low, re_p, pltpu.roll(im_p, CH_DEV, 1))
+                second = jnp.where(low, pltpu.roll(re_p, CH_DEV, 1), im_p)
+                at = GROUP * odd + 2 * half
+                staged[pl.ds(at, HALF, stride=2 * GROUP), :] = first
+                staged[pl.ds(at + 1, HALF, stride=2 * GROUP), :] = second
         sent[:, i] = staged[...].reshape(F, GROUP, 128).astype(BF16)
 
     pl.semaphore_wait(barrier, DEVICES - 1)
@@ -325,6 +340,12 @@
     fold_ref[...] = lagged[end : end + ROWS]
 
 
+def hand_over(near_in, fold_in, near_out, fold_out):
+    factor = 1.0 / math.sqrt(F * WINDOWS)
+    near_out[...] = near_in[...] * factor
+    fold_out[...] = fold_in[...] * factor
+
+
 def local(traces, quality, fold_block, fold_offset):
     vmem = pl.BlockSpec(memory_space=pltpu.VMEM)
     hbm = pl.BlockSpec(memory_space=pltpu.MemorySpace.HBM)
@@ -345,8 +366,8 @@
             pltpu.VMEM((1, CHANNELS), jnp.int32),
             pltpu.VMEM(phases.shape, F32),
             pltpu.VMEM(inverse.shape, BF16),
-            pltpu.VMEM((2 * F, L), BF16),
-            pltpu.VMEM((F + 16, LANES), F32),
+            pltpu.VMEM((2, F, L // 2), BF16),
+            pltpu.VMEM((2, HALF + 16, LANES), F32),
             pltpu.VMEM((F * GROUP, 128), F32),
             pltpu.VMEM((DEVICES, CHUNKS, GROUP, 128), BF16),
             pltpu.VMEM((DEVICES, CHUNKS, GROUP, 128), BF16),
@@ -379,8 +400,21 @@
         phases,
         inverse,
     )
-    factor = 1.0 / math.sqrt(F * WINDOWS)
-    return near_lags * factor, fold_lags * factor
+    shapes = tuple(jax.ShapeDtypeStruct(a.shape, a.dtype) for a in (near_lags, fold_lags))
+    return pl.pallas_call(
+        hand_over,
+        grid=(2,),
+        out_shape=shapes,
+        in_specs=[
+            pl.BlockSpec((ROWS // 2, REACH, NLAG), lambda i: (i, 0, 0)),
+            pl.BlockSpec((ROWS, NLAG), lambda i: (0, 0)),
+        ],
+        out_specs=(
+            pl.BlockSpec((ROWS // 2, REACH, NLAG), lambda i: (i, 0, 0)),
+            pl.BlockSpec((ROWS, NLAG), lambda i: (0, 0)),
+        ),
+        compiler_params=pltpu.CompilerParams(vmem_limit_bytes=60 << 20),
+    )(near_lags, fold_lags)
 
 
 def solution(mesh):

time: 64.1 us -> 59.1 us (0.922)
  other arithmetic: 3.18 us -> 0 us
  Pallas kernels: 60.1 us -> 58.3 us
    pallas_call x1, Pallas kernels: 60.1 us -> 56.5 us  [local(): pl.pallas_call(kernel, out_shape=(jax.ShapeDtypeStruct((ROWS, REACH, NLAG...]
    mul x2 -> x0, other arithmetic: 3.18 us -> none  [local(): return (near_lags * factor, fold_lags * factor)]
    pallas_call x0 -> x1, Pallas kernels: none -> 1.79 us  [local(): pl.pallas_call(hand_over, grid=(2,), out_shape=shapes, in_specs=[pl.Block...]
where the time goes in v4:
time: 59.1 us; the launch traced here: 59 us
  Pallas kernels  58.3 us (99%)
  between operations  0.64 us (1%)
    pallas_call x1, Pallas kernels, local(): pl.pallas_call(kernel, out_shape=(jax.ShapeDtypeStruct((ROWS, REACH, NLAG...  56.5 us
    pallas_call x1, Pallas kernels, local(): pl.pallas_call(hand_over, grid=(2,), out_shape=shapes, in_specs=[pl.Block...  1.79 us

profile of v4, /device:TPU:1, one launch (start us, length us, event | category | flops | bytes accessed | tf_op | source)
XLA Modules:
  0.0 59.0 jit_solution(5220327982135164865)
XLA Ops:
  0.6 56.5 %shard_map.77 = (f32[8,64,256]{2,1,0:T(8,128)}, f32[8,256]{1,0:T(8,128)}) custom-call(bf16[768,4096]{1,0:T(8,128)(2,1)} %bitcast.4, s32[1,64]{1,0:T(1,128)} %bitcast.7, s32[1,2048]{1,0:T(1,128)} %bitcast.5, s32[1,2048]{1,0:T(1,128)} %bitcast.6, f32[256,384]{1,0:T(8,128)} %constant.4.clone.phase_hbm, bf16[4,256,256]{2,1,0:T(8,128)(2,1)} %constant.5.clone.inverse_hbm), custom_call_target="tpu_custom_call" | custom-call | tf_op jit(solution)/shard_map/pallas_call | solution.py:354
  57.2 1.8 %shard_map.78 = (f32[8,64,256]{2,1,0:T(8,128)}, f32[8,256]{1,0:T(8,128)}) custom-call(f32[8,64,256]{2,1,0:T(8,128)} %get-tuple-element.4.near_in, f32[8,256]{1,0:T(8,128)} %get-tuple-element.5.fold_in), custom_call_target="tpu_custom_call" | custom-call | tf_op jit(solution)/shard_map/pallas_call | solution.py:404

commit v5 on v4

--- a/solution.py
+++ b/solution.py
@@ -120,8 +120,11 @@
         cosines = (fine_cos * cos_b - fine_sin * sin_b).astype(BF16)
         sines = (-fine_sin * cos_b - fine_cos * sin_b).astype(BF16)
         for odd in range(2):
-            table[odd, 0:HALF, lanes] = cosines[odd * HALF : (odd + 1) * HALF]
-            table[odd, HALF:F, lanes] = sines[odd * HALF : (odd + 1) * HALF]
+            later = slice(L // 2 + block * STEP, L // 2 + (block + 1) * STEP)
+            for row, part in ((0, cosines), (HALF, sines)):
+                part = part[odd * HALF : (odd + 1) * HALF]
+                table[odd, row : row + HALF, lanes] = part
+                table[odd, row : row + HALF, later] = -part if odd else part
     edge = jnp.zeros((8, LANES), F32)
     for odd in range(2):
         energy[odd, 0:8, :] = edge
@@ -134,10 +137,9 @@
     over_lanes = (((1,), (1,)), ((), ()))
     for i in range(CHUNKS):
         x_copies[i].wait()
-        early, late = xs[i, :, 0 : L // 2], xs[i, :, L // 2 : L]
         parts, powers = [], []
-        for odd, mixed in enumerate((early + late, early - late)):
-            spectra = lax.dot_general(table[odd], mixed, over_lanes, preferred_element_type=F32)
+        for odd in range(2):
+            spectra = lax.dot_general(table[odd], xs[i], over_lanes, preferred_element_type=F32)
             re, im = spectra[0:HALF], spectra[HALF:F]
             power = re * re + im * im
             energy[odd, 8 : 8 + HALF, :] = power
@@ -366,7 +368,7 @@
             pltpu.VMEM((1, CHANNELS), jnp.int32),
             pltpu.VMEM(phases.shape, F32),
             pltpu.VMEM(inverse.shape, BF16),
-            pltpu.VMEM((2, F, L // 2), BF16),
+            pltpu.VMEM((2, F, L), BF16),
             pltpu.VMEM((2, HALF + 16, LANES), F32),
             pltpu.VMEM((F * GROUP, 128), F32),
             pltpu.VMEM((DEVICES, CHUNKS, GROUP, 128), BF16),

time: 59.1 us -> 58.9 us (level)
  no operation moved by 1% of the time
where the time goes in v5:
time: 58.9 us; the launch traced here: 58.8 us
  Pallas kernels  58.2 us (99%)
  between operations  0.64 us (1%)
    pallas_call x1, Pallas kernels, local(): pl.pallas_call(kernel, out_shape=(jax.ShapeDtypeStruct((ROWS, REACH, NLAG...  56.4 us
    pallas_call x1, Pallas kernels, local(): pl.pallas_call(hand_over, grid=(2,), out_shape=shapes, in_specs=[pl.Block...  1.79 us

profile of v5, /device:TPU:1, one launch (start us, length us, event | category | flops | bytes accessed | tf_op | source)
XLA Modules:
  0.0 58.8 jit_solution(9965747506840693506)
XLA Ops:
  0.6 56.4 %shard_map.77 = (f32[8,64,256]{2,1,0:T(8,128)}, f32[8,256]{1,0:T(8,128)}) custom-call(bf16[768,4096]{1,0:T(8,128)(2,1)} %bitcast.4, s32[1,64]{1,0:T(1,128)} %bitcast.7, s32[1,2048]{1,0:T(1,128)} %bitcast.5, s32[1,2048]{1,0:T(1,128)} %bitcast.6, f32[256,384]{1,0:T(8,128)} %constant.4.clone.phase_hbm, bf16[4,256,256]{2,1,0:T(8,128)(2,1)} %constant.5.clone.inverse_hbm), custom_call_target="tpu_custom_call" | custom-call | tf_op jit(solution)/shard_map/pallas_call | solution.py:356
  57.0 1.8 %shard_map.78 = (f32[8,64,256]{2,1,0:T(8,128)}, f32[8,256]{1,0:T(8,128)}) custom-call(f32[8,64,256]{2,1,0:T(8,128)} %get-tuple-element.4.near_in, f32[8,256]{1,0:T(8,128)} %get-tuple-element.5.fold_in), custom_call_target="tpu_custom_call" | custom-call | tf_op jit(solution)/shard_map/pallas_call | solution.py:406

commit v6 on v5

--- a/solution.py
+++ b/solution.py
@@ -310,10 +310,6 @@
     band_copies = all_of(band, band_in, band_send, band_recv, DEVICES - 1)
     band_copies.wait_send()
     band_copies.wait_recv()
-    fold_copies.wait_send()
-    relay_copies = all_of(folded_in, folded_in, relay_send, relay_recv, N_WIN - 1)
-    relay_copies.wait_send()
-    relay_copies.wait_recv()
     own_band.wait()
     small_copies[4].wait()
 
@@ -323,6 +319,22 @@
         at = (ROWS - 1 - r) * REACH
         lag_in[0, at : at + REACH, :] = turned[:REACH].astype(BF16)
         lag_in[1, at : at + REACH, :] = turned[REACH:].astype(BF16)
+    def transform(first, count):
+        total = jnp.zeros((count, NLAG), F32)
+        for part in range(2):
+            for half in range(2):
+                rows = lag_in[part, first : first + count, :]
+                total += jnp.dot(rows, inverse[2 * part + half], preferred_element_type=F32)
+        return total
+
+    end = ROWS * REACH
+    near_ref[...] = transform(0, end).reshape(ROWS, REACH, NLAG)
+
+    fold_copies.wait_send()
+    relay_copies = all_of(folded_in, folded_in, relay_send, relay_recv, N_WIN - 1)
+    relay_copies.wait_send()
+    relay_copies.wait_recv()
+
     flat_fold[...] = folded_in[...].astype(F32).reshape(DEVICES * 2, 128)
     for w in range(N_WIN):
         rows = flat_fold[pl.ds(2 * N_CHAN * w, N_CHAN, stride=2), :]
@@ -330,16 +342,10 @@
     turned_fold[...] = by_bin[...].T
     own = pl.multiple_of(win * ROWS, ROWS)
     pad = jnp.zeros((ROWS, F), F32)
-    end = ROWS * REACH
     for part in range(2):
         mine = turned_fold[pl.ds(part * CH_DEV + own, ROWS), :]
         lag_in[part, end : end + 2 * ROWS, :] = jnp.concatenate([mine, pad], axis=0).astype(BF16)
-    lagged = jnp.zeros((end + 2 * ROWS, NLAG), F32)
-    for part in range(2):
-        for half in range(2):
-            lagged += jnp.dot(lag_in[part], inverse[2 * part + half], preferred_element_type=F32)
-    near_ref[...] = lagged[:end].reshape(ROWS, REACH, NLAG)
-    fold_ref[...] = lagged[end : end + ROWS]
+    fold_ref[...] = transform(end, 2 * ROWS)[:ROWS]
 
 
 def hand_over(near_in, fold_in, near_out, fold_out):

time: 58.9 us -> 58.4 us (level)
  Pallas kernels: 58.2 us -> 57.6 us
where the time goes in v6:
time: 58.4 us; the launch traced here: 58.2 us
  Pallas kernels  57.6 us (99%)
  between operations  0.64 us (1%)
    pallas_call x1, Pallas kernels, local(): pl.pallas_call(kernel, out_shape=(jax.ShapeDtypeStruct((ROWS, REACH, NLAG...  55.8 us
    pallas_call x1, Pallas kernels, local(): pl.pallas_call(hand_over, grid=(2,), out_shape=shapes, in_specs=[pl.Block...  1.79 us

profile of v6, /device:TPU:1, one launch (start us, length us, event | category | flops | bytes accessed | tf_op | source)
XLA Modules:
  0.0 58.2 jit_solution(12757241578064588535)
XLA Ops:
  0.6 55.8 %shard_map.77 = (f32[8,64,256]{2,1,0:T(8,128)}, f32[8,256]{1,0:T(8,128)}) custom-call(bf16[768,4096]{1,0:T(8,128)(2,1)} %bitcast.4, s32[1,64]{1,0:T(1,128)} %bitcast.7, s32[1,2048]{1,0:T(1,128)} %bitcast.5, s32[1,2048]{1,0:T(1,128)} %bitcast.6, f32[256,384]{1,0:T(8,128)} %constant.4.clone.phase_hbm, bf16[4,256,256]{2,1,0:T(8,128)(2,1)} %constant.5.clone.inverse_hbm), custom_call_target="tpu_custom_call" | custom-call | tf_op jit(solution)/shard_map/pallas_call | solution.py:362
  56.5 1.8 %shard_map.78 = (f32[8,64,256]{2,1,0:T(8,128)}, f32[8,256]{1,0:T(8,128)}) custom-call(f32[8,64,256]{2,1,0:T(8,128)} %get-tuple-element.4.near_in, f32[8,256]{1,0:T(8,128)} %get-tuple-element.5.fold_in), custom_call_target="tpu_custom_call" | custom-call | tf_op jit(solution)/shard_map/pallas_call | solution.py:412
